TPU v7x, 32 devices: a whole 2x2x4 slice. The times are simulated.
32 devices in a mesh: groups: 1, ctx: 2 (over x), fsdp: 16 (over z, y, core).
Axes of the slice: x: 2, y: 2, z: 4, core: 2. Of those that a mesh axis runs over, the one named last changes fastest.
Arguments:
- tokens: bfloat16 [16, 256, 3072], P(('groups', 'fsdp'), 'ctx'), may hold values from -600 to 600
- trace_index: int32 [16, 256], P(('groups', 'fsdp'), 'ctx'), may hold values from 0 to 1, never falling along the last dimension, each value on 1 to 192 neighbouring positions
- input_norm_scale: bfloat16 [3072], replicated, may hold values from 0.099609375 to 1.8984375
- query_weight: bfloat16 [3072, 2048], P('fsdp'), may hold values from -0.109375 to 0.109375
- key_weight: bfloat16 [3072, 1024], P('fsdp'), may hold values from -0.109375 to 0.109375
- value_weight: bfloat16 [3072, 1024], P('fsdp'), may hold values from -0.109375 to 0.109375
- query_down_weight: bfloat16 [3072, 16], replicated, may hold values from -0.109375 to 0.109375
- query_up_weight: bfloat16 [16, 2048], replicated, may hold values from -1.5 to 1.5
- value_down_weight: bfloat16 [3072, 16], replicated, may hold values from -0.109375 to 0.109375
- value_up_weight: bfloat16 [16, 1024], replicated, may hold values from -1.5 to 1.5
- output_gradient: bfloat16 [16, 256, 2048], P(('groups', 'fsdp'), 'ctx'), may hold values from -24 to 24
Outputs:
- grad_a_query: float32 [3072, 16], P('groups')
- grad_b_query: float32 [16, 2048], P('groups')
- grad_a_value: float32 [3072, 16], P('groups')
- grad_b_value: float32 [16, 1024], P('groups')
Inputs may be any that keep to these rules, and one draw needn't show every extreme that they name: `trace_index`: ids never fall along a sequence; one trace holds at most 192 positions.
All inputs are finite; a program needn't handle non-finite values.
Results may differ from a plain program's by a relative error of at most 0.013.
Values may be sent and summed in bfloat16 or wider, within the bound.
A program may use at most 128 MiB of HBM per device.

v0:
```python
import math
import jax
import jax.numpy as jnp
from jax import lax
from jax.sharding import PartitionSpec as P

HEAD_SIZE = 128
CAP = 50.0
QSCALE = 1.0 / 12.0
ADAPTER_NAME = 0.5
EPS = 1e-06


def shifted(value, axis, by):
    devices = lax.axis_size(axis)
    pairs = [(i, i + by) for i in range(devices) if 0 <= i + by < devices]
    return lax.ppermute(value, axis, pairs)


def normed_rows(values, gain):
    flt = values.astype(jnp.float32)
    meansq = jnp.mean(flt * flt, axis=-1, keepdims=True)
    return (flt * lax.rsqrt(meansq + EPS) * gain.astype(jnp.float32)).astype(jnp.bfloat16)


def add_rows(left, piece):
    return jnp.dot(left, piece, preferred_element_type=jnp.float32)


def attend_head(operands, mask):
    q_head, k_head, v_head, g_head = operands
    s = jnp.einsum("igd,jd->gij", q_head, k_head, preferred_element_type=jnp.float32) * QSCALE
    t = jnp.tanh(s / CAP)
    capped = CAP * t
    expo = jnp.where(mask[None], jnp.exp(capped), jnp.float32(0.0))
    weights = expo / jnp.sum(expo, axis=-1, keepdims=True)
    weights16 = weights.astype(jnp.bfloat16)
    attended = jnp.einsum("gij,jd->igd", weights16, v_head, preferred_element_type=jnp.float32)
    dweight = jnp.einsum("igd,jd->gij", g_head, v_head, preferred_element_type=jnp.float32)
    delta = jnp.sum(g_head.astype(jnp.float32) * attended, axis=-1).T
    dscore = (weights * (dweight - delta[..., None]) * (1.0 - t * t) * QSCALE).astype(jnp.bfloat16)
    query_gradient = jnp.einsum(
        "gij,jd->igd", dscore, k_head, preferred_element_type=jnp.float32
    ).astype(jnp.bfloat16)
    value_gradient = jnp.einsum(
        "gij,igd->jd", weights16, g_head, preferred_element_type=jnp.float32
    )
    return (query_gradient, value_gradient)


def partial_attend(mask):

    def run_head(operands):
        return attend_head(operands, mask)

    return run_head


def on_device(
    tokens,
    trace_index,
    input_norm_scale,
    query_weight,
    key_weight,
    value_weight,
    query_down_weight,
    query_up_weight,
    value_down_weight,
    value_up_weight,
    output_gradient,
):
    window_width = tokens.shape[1]
    feats = tokens.shape[2]
    heads_kv = key_weight.shape[1] // HEAD_SIZE
    heads_q = query_weight.shape[1] // HEAD_SIZE
    head_group = heads_q // heads_kv
    normalized_input = normed_rows(tokens.reshape(window_width, feats), input_norm_scale)
    seg_own = trace_index.reshape(window_width).astype(jnp.bfloat16)
    seg_parts = []

    def add_keyval(piece):
        return add_rows(normalized_input, piece)

    query_frozen = add_rows(
        normalized_input, lax.all_gather(query_weight, "fsdp", axis=0, tiled=True)
    )
    k_base = add_keyval(lax.all_gather(key_weight, "fsdp", axis=0, tiled=True))
    value_frozen = add_keyval(lax.all_gather(value_weight, "fsdp", axis=0, tiled=True))
    query_reduced = jnp.dot(
        normalized_input, query_down_weight, preferred_element_type=jnp.float32
    ).astype(jnp.bfloat16)
    reduced_rows = jnp.dot(
        normalized_input, value_down_weight, preferred_element_type=jnp.float32
    ).astype(jnp.bfloat16)
    query_matrix = (
        query_frozen
        + ADAPTER_NAME * jnp.dot(query_reduced, query_up_weight, preferred_element_type=jnp.float32)
    ).astype(jnp.bfloat16)
    key_rows = k_base.astype(jnp.bfloat16)
    value_rows = (
        value_frozen
        + ADAPTER_NAME * jnp.dot(reduced_rows, value_up_weight, preferred_element_type=jnp.float32)
    ).astype(jnp.bfloat16)
    key_parts = []
    value_parts = []
    for distance in (2, 1):
        key_prev, value_prev, seg_prev = shifted((key_rows, value_rows, seg_own), "ctx", distance)
        key_parts.append(key_prev)
        value_parts.append(value_prev)
        seg_parts.append(seg_prev)
    keys_all = jnp.concatenate(key_parts + [key_rows], 0)
    values_all = jnp.concatenate(value_parts + [value_rows], 0)
    seg_keys = jnp.concatenate(seg_parts + [seg_own], 0)
    pos_q = jnp.arange(window_width, dtype=jnp.int32)[:, None]
    pos_k = jnp.arange(3 * window_width, dtype=jnp.int32)[None, :]
    position = lax.axis_index("ctx")
    mask = (
        (pos_k > pos_q)
        & (pos_k <= pos_q + 2 * window_width)
        & (seg_keys[None, :] == seg_own[:, None])
    )
    mask = mask & (
        (pos_k >= 2 * window_width) | (pos_k >= window_width) & (position >= 1) | (position >= 2)
    )
    q_heads = jnp.moveaxis(
        query_matrix.reshape(window_width, heads_kv, head_group, HEAD_SIZE), 1, 0
    )
    g_heads = jnp.moveaxis(
        output_gradient.reshape(window_width, heads_kv, head_group, HEAD_SIZE), 1, 0
    )
    k_heads = jnp.moveaxis(keys_all.reshape(3 * window_width, heads_kv, HEAD_SIZE), 1, 0)
    v_heads = jnp.moveaxis(values_all.reshape(3 * window_width, heads_kv, HEAD_SIZE), 1, 0)
    dquery_heads, dvalue_heads = lax.map(partial_attend(mask), (q_heads, k_heads, v_heads, g_heads))
    query_gradient = jnp.moveaxis(dquery_heads, 0, 1).reshape(window_width, heads_q * HEAD_SIZE)
    dvalue_triple = jnp.moveaxis(dvalue_heads, 0, 1).reshape(3 * window_width, heads_kv * HEAD_SIZE)
    value_gradient = dvalue_triple[2 * window_width :]
    for distance in (1, 2):
        begin = (2 - distance) * window_width
        value_gradient = value_gradient + shifted(
            dvalue_triple[begin : begin + window_width], "ctx", -distance
        )
    query_backward = jnp.dot(
        query_gradient, query_up_weight.T, preferred_element_type=jnp.float32
    ).astype(jnp.bfloat16)
    value_backward = jnp.dot(
        value_gradient, value_up_weight.astype(jnp.float32).T, precision=lax.Precision.HIGHEST
    )
    part_aq = jnp.dot(normalized_input.T, query_backward, preferred_element_type=jnp.float32)
    part_bq = jnp.dot(query_reduced.T, query_gradient, preferred_element_type=jnp.float32)
    part_av = jnp.dot(
        normalized_input.astype(jnp.float32).T, value_backward, precision=lax.Precision.HIGHEST
    )
    part_bv = jnp.dot(
        reduced_rows.astype(jnp.float32).T, value_gradient, precision=lax.Precision.HIGHEST
    )
    sum_aq, sum_bq, sum_av, sum_bv = lax.psum((part_aq, part_bq, part_av, part_bv), ("ctx", "fsdp"))
    token_total = lax.axis_size("ctx") * lax.axis_size("fsdp") * window_width
    coefficient = ADAPTER_NAME / math.sqrt(token_total)
    return (sum_aq * coefficient, sum_bq * coefficient, sum_av * coefficient, sum_bv * coefficient)


def solution(mesh):
    return jax.shard_map(
        on_device,
        mesh=mesh,
        in_specs=(
            P(("groups", "fsdp"), "ctx", None),
            P(("groups", "fsdp"), "ctx"),
            P(),
            P("fsdp", None),
            P("fsdp", None),
            P("fsdp", None),
            P(),
            P(),
            P(),
            P(),
            P(("groups", "fsdp"), "ctx", None),
        ),
        out_specs=(P("groups", None), P("groups", None), P("groups", None), P("groups", None)),
        check_vma=False,
    )
```

profile of v0, /device:TPU:0, one launch (start us, length us, event | category | flops | bytes accessed | tf_op | source)
XLA Modules:
  0.0 444.9 jit_solution(15233795654485202083)
XLA Ops:
  7.3 0.7 all-gather.8.cloned.1.call-update
  8.0 0.7 all-gather.4.cloned.1.call-update
  8.8 0.7 all-gather.6.cloned.1.call-update
  9.5 0.7 collective-permute-start.2
  10.2 0.5 iota_add_fusion
  11.0 0.4 convolution_convert_fusion.2
  11.3 1.0 convolution_convert_fusion.3
  12.4 62.1 %all-gather.8.cloned.1.call-done = bf16[3072,1024]{1,0:T(8,128)(2,1)} async-done(((bf16[192,1024]{1,0:T(8,128)(2,1)}), bf16[3072,1024]{1,0:T(8,128)(2,1)}) %all-gather.8.cloned.1.call-update) | async-done | bytes 6291472 | tf_op jit(solution)/shard_map/all_gather | solution.py:88
  74.5 3.8 fusion.71
  78.6 0.8 collective-permute-start.4
  79.4 3.4 collective-permute-start.5
  82.8 54.1 %all-gather.4.cloned.1.call-done = bf16[3072,1024]{1,0:T(8,128)(2,1)} async-done(((bf16[192,1024]{1,0:T(8,128)(2,1)}), bf16[3072,1024]{1,0:T(8,128)(2,1)}) %all-gather.4.cloned.1.call-update) | async-done | bytes 6291472 | tf_op jit(solution)/shard_map/all_gather | solution.py:87
  136.9 3.8 convolution_convert_fusion
  140.7 0.7 collective-permute-start
  141.4 4.1 collective-permute-start.1
  145.5 0.5 fusion.65
  146.0 1.3 collective-permute-start.3
  147.6 3.2 collective-permute-done.3
  151.0 2.0 bitcast_bitcast_fusion.1
  153.0 85.4 %all-gather.6.cloned.1.call-done = bf16[3072,2048]{1,0:T(8,128)(2,1)} async-done(((bf16[192,2048]{1,0:T(8,128)(2,1)}), bf16[3072,2048]{1,0:T(8,128)(2,1)}) %all-gather.6.cloned.1.call-update) | async-done | bytes 12582928 | tf_op jit(solution)/shard_map/all_gather | solution.py:85
  238.3 6.4 %fusion.74 = f32[128,2048]{1,0:T(8,128)S(1)} fusion(bf16[3072,2048]{1,0:T(8,128)(2,1)} %all-gather.6.cloned.1.call-done, bf16[1,128,3072]{2,1,0:T(8,128)(2,1)S(1)} %copy-done.1, f32[3072]{0:T(1024)S(1)} %convert_element_type.72, f32[128]{0:T(128)} %copy-done.14), kind=kOutput, calls=%fused_computation.95 | convolution fusion | flops 1612185600 | bytes 14430720 | tf_op jit(solution)/shard_map/dot_general | solution.py:27
  245.5 0.9 copy.40
  246.4 38.3 %while.15 = (s32[]{:T(128)}, bf16[8,128,2,128]{1,3,2,0:T(8,128)(2,1)}, f32[8,384,128]{1,2,0:T(8,128)}, bf16[8,384,128]{2,1,0:T(8,128)(2,1)}, bf16[8,128,2,128]{3...) while((s32[]{:T(128)}, ...), condition=%wide.region_4.5_spmd.clone, body=%wide.region_1.4_spmd.clone.sunk | while | flops 128122368 | bytes 3156989 | solution.py:133
  246.6 1.2 fusion.122
  247.9 0.9 fusion.126
  248.9 0.4 fusion.124
  249.3 1.9 fusion.125
  251.4 1.2 fusion.122
  252.7 0.9 fusion.126
  253.7 0.4 fusion.124
  254.1 1.9 fusion.125
  256.2 1.2 fusion.122
  257.5 0.9 fusion.126
  258.5 0.4 fusion.124
  258.9 1.9 fusion.125
  261.0 1.2 fusion.122
  262.3 0.9 fusion.126
  263.7 1.9 fusion.125
  265.8 1.2 fusion.122
  267.1 0.9 fusion.126
  268.5 1.9 fusion.125
  270.6 1.2 fusion.122
  271.9 0.9 fusion.126
  273.3 1.9 fusion.125
  275.3 1.2 fusion.122
  276.6 0.9 fusion.126
  278.0 1.9 fusion.125
  280.1 1.2 fusion.122
  281.4 0.9 fusion.126
  282.8 1.9 fusion.125
  284.7 1.5 fusion.77
  286.3 1.3 collective-permute-start.6
  287.6 1.5 collective-permute-start.7
  289.0 0.9 fusion.78
  289.9 2.3 fusion.62
  292.2 10.1 %collective-permute-done.6 = f32[128,1024]{0,1:T(8,128)S(1)} collective-permute-done((f32[128,1024]{0,1:T(8,128)S(1)}, f32[128,1024]{0,1:T(8,128)S(1)}, u32[]{:S(2)}, u32[]{:S(2)}) %collective-permute-start.6) | collective-permute-done | bytes 524320 | tf_op jit(solution)/shard_map/ppermute | solution.py:17
  302.3 1.1 fusion.63
  303.4 0.6 fusion.79
  304.0 1.0 fusion.80
  305.0 1.3 fusion.67
  306.2 127.3 %all-reduce.3.cloned.1.call-done = (f32[3072,16]{0,1:T(8,128)}, f32[16,2048]{1,0:T(8,128)}, f32[3072,16]{0,1:T(8,128)}, f32[16,1024]{1,0:T(8,128)}) async-done(((f32[3072,16]{0,1:T(8,128)}, f32[16,2048]{1,0:T(8,128)}, f32[3072,16]{0,1:T(8,128)}, f32[16,1024]{1,0:T(8,128)}), (f32[3072,16]{0,1:T(8,128)}, f32[16,2048]{1,0:T(8,128)}, f32[3072,16]{0,1:T(8,128)}, ...) | async-done | bytes 589840 | tf_op jit(solution)/shard_map/psum | solution.py:156
  433.5 1.6 broadcast_multiply_fusion.2
  435.1 1.5 broadcast_multiply_fusion.3
  436.5 1.8 broadcast_multiply_fusion
  (98 shorter events, 6.9 us)
Async XLA Ops:
  7.2 3.8 copy-start
  7.2 2.3 copy-start.18
  7.2 3.0 copy-start.16
  7.2 3.5 copy-start.1
  7.2 67.2 %all-gather.8.cloned.1.call-start = ((), (), s32[]{:S(2)}) async-start(), calls=%async_computation.2 | async-start | bytes 6684672 | tf_op jit(solution)/shard_map/all_gather | solution.py:88
  7.9 128.9 %all-gather.4.cloned.1.call-start = ((), (), s32[]{:S(2)}) async-start(), calls=%async_computation | async-start | bytes 6684672 | tf_op jit(solution)/shard_map/all_gather | solution.py:87
  8.7 2.7 copy-start.17
  8.7 229.6 %all-gather.6.cloned.1.call-start = ((), (), s32[]{:S(2)}) async-start(), calls=%async_computation.1 | async-start | bytes 13369344 | tf_op jit(solution)/shard_map/all_gather | solution.py:85
  9.4 424.1 %all-reduce.3.cloned.1.call-start = ((), (), s32[]{:S(2)}) async-start(), calls=%async_computation.3 | async-start | bytes 1179648 | tf_op jit(solution)/shard_map/psum | solution.py:156
  9.5 141.3 %copy-start.6 = (bf16[128]{0:T(256)(128)(2,1)}, bf16[128]{0:T(256)(128)(2,1)S(1)}, u32[]{:S(2)}) copy-start(bf16[128]{0:T(256)(128)(2,1)S(1)} %convert_bitcast_fusion) | copy-start | bytes 772
  9.5 136.5 %collective-permute-start.2 = (bf16[128]{0:T(256)(128)(2,1)S(1)}, bf16[128]{0:T(256)(128)(2,1)S(1)}, u32[]{:S(2)}, u32[]{:S(2)}) collective-permute-start(bf16[128]{0:T(256)(128)(2,1)S(1)} %convert_bitcast_fusion), channel_id=1, source_target_pairs={} | collective-permute-start | bytes 776 | tf_op jit(solution)/shard_map/ppermute | solution.py:17
  11.0 125.9 %copy-start.14 = (f32[128]{0:T(128)}, f32[128]{0:T(128)S(1)}, u32[]{:S(2)}) copy-start(f32[128]{0:T(128)S(1)} %add_rsqrt_fusion) | copy-start | bytes 1540
  11.3 66.9 %copy-start.8 = (bf16[128,16]{0,1:T(8,128)(2,1)}, bf16[128,16]{0,1:T(8,128)(2,1)S(1)}, u32[]{:S(2)}) copy-start(bf16[128,16]{0,1:T(8,128)(2,1)S(1)} %convolution_convert_fusion.2) | copy-start | bytes 12292
  12.4 65.9 %copy-start.4 = (bf16[16,1024]{1,0:T(8,128)(2,1)S(1)}, bf16[16,1024]{1,0:T(8,128)(2,1)}, u32[]{:S(2)}) copy-start(bf16[16,1024]{1,0:T(8,128)(2,1)} %param.22) | copy-start | bytes 98308
  78.5 68.8 %copy-start.3 = (bf16[1,128,2048]{2,1,0:T(8,128)(2,1)S(1)}, bf16[1,128,2048]{2,1,0:T(8,128)(2,1)}, u32[]{:S(2)}) copy-start(bf16[1,128,2048]{2,1,0:T(8,128)(2,1)} %param.23) | copy-start | bytes 1572868
  78.6 72.2 %collective-permute-start.4 = (bf16[128,1024]{1,0:T(8,128)(2,1)S(1)}, bf16[128,1024]{1,0:T(8,128)(2,1)S(1)}, u32[]{:S(2)}, u32[]{:S(2)}) collective-permute-start(bf16[128,1024]{1,0:T(8,128)(2,1)S(1)} %fusion.61), channel_id=1, source_target_pairs={} | collective-permute-start | bytes 786440 | tf_op jit(solution)/shard_map/ppermute | solution.py:17
  79.4 71.4 %collective-permute-start.5 = (bf16[128,1024]{1,0:T(8,128)(2,1)S(1)}, bf16[128,1024]{1,0:T(8,128)(2,1)S(1)}, u32[]{:S(2)}, u32[]{:S(2)}) collective-permute-start(bf16[128,1024]{1,0:T(8,128)(2,1)S(1)} %fusion.61), channel_id=1, source_target_pairs={{0,16},{1,17},{2,18},{3,19},{4,20},{5,21},{6,22},{7,23},{8,24},{9,... | collective-permute-start | bytes 786440 | tf_op jit(solution)/shard_map/ppermute | solution.py:17
  140.7 10.2 %collective-permute-start = (bf16[128,1024]{1,0:T(8,128)(2,1)S(1)}, bf16[128,1024]{1,0:T(8,128)(2,1)S(1)}, u32[]{:S(2)}, u32[]{:S(2)}) collective-permute-start(bf16[128,1024]{1,0:T(8,128)(2,1)S(1)} %convolution_convert_fusion), channel_id=1, source_target_pairs={} | collective-permute-start | bytes 786440 | tf_op jit(solution)/shard_map/ppermute | solution.py:17
  141.4 9.6 %collective-permute-start.1 = (bf16[128,1024]{1,0:T(8,128)(2,1)S(1)}, bf16[128,1024]{1,0:T(8,128)(2,1)}, u32[]{:S(2)}, u32[]{:S(2)}) collective-permute-start(bf16[128,1024]{1,0:T(8,128)(2,1)S(1)} %convolution_convert_fusion), channel_id=1, source_target_pairs={{0,16},{1,17},{2,18},{3,19},{4,20},{5,21},{6,22},{7,23},{8,24},{9,... | collective-permute-start | bytes 786440 | tf_op jit(solution)/shard_map/ppermute | solution.py:17
  146.0 4.8 %collective-permute-start.3 = (bf16[128]{0:T(256)(128)(2,1)S(1)}, bf16[128]{0:T(256)(128)(2,1)S(1)}, u32[]{:S(2)}, u32[]{:S(2)}) collective-permute-start(bf16[128]{0:T(256)(128)(2,1)S(1)} %convert_bitcast_fusion), channel_id=1, source_target_pairs={{0,16},{1,17},{2,18},{3,19},{4,20},{5,21},{6,22},{7,23},{8,24},{9,... | collective-permute-start | bytes 776 | tf_op jit(solution)/shard_map/ppermute | solution.py:17
  153.0 91.8 %copy-start.5 = (bf16[16,2048]{1,0:T(8,128)(2,1)S(1)}, bf16[16,2048]{1,0:T(8,128)(2,1)}, u32[]{:S(2)}) copy-start(bf16[16,2048]{1,0:T(8,128)(2,1)} %param.20) | copy-start | bytes 196612
  153.0 91.8 %copy-start.10 = (bf16[128,16]{0,1:T(8,128)(2,1)S(1)}, bf16[128,16]{0,1:T(8,128)(2,1)}, u32[]{:S(2)}) copy-start(bf16[128,16]{0,1:T(8,128)(2,1)} %convolution_convert_fusion.3) | copy-start | bytes 12292
  244.8 1.7 copy-start.7
  244.8 1.6 copy-start.12
  244.8 1.6 copy-start.13
  284.7 4.3 copy-start.2
  284.7 4.3 copy-start.11
  284.7 5.2 %copy-start.15 = (f32[128]{0:T(128)S(1)}, f32[128]{0:T(128)}, u32[]{:S(2)}) copy-start(f32[128]{0:T(128)} %copy-done.14) | copy-start | bytes 1540
  286.3 16.0 %collective-permute-start.6 = (f32[128,1024]{0,1:T(8,128)S(1)}, f32[128,1024]{0,1:T(8,128)S(1)}, u32[]{:S(2)}, u32[]{:S(2)}) collective-permute-start(f32[128,1024]{0,1:T(8,128)S(1)} %bitcast.193), channel_id=1, source_target_pairs={{16,0},{17,1},{18,2},{19,3},{20,4},{21,5},{22,6},{23,7},{24,8},{25... | collective-permute-start | bytes 1572872 | tf_op jit(solution)/shard_map/ppermute | solution.py:17
  287.6 14.7 %collective-permute-start.7 = (f32[128,1024]{0,1:T(8,128)S(1)}, f32[128,1024]{0,1:T(8,128)}, u32[]{:S(2)}, u32[]{:S(2)}) collective-permute-start(f32[128,1024]{0,1:T(8,128)S(1)} %bitcast.192), channel_id=1, source_target_pairs={} | collective-permute-start | bytes 1572872 | tf_op jit(solution)/shard_map/ppermute | solution.py:17
  292.2 11.8 %copy-start.9 = (bf16[128,16]{0,1:T(8,128)(2,1)S(1)}, bf16[128,16]{0,1:T(8,128)(2,1)}, u32[]{:S(2)}) copy-start(bf16[128,16]{0,1:T(8,128)(2,1)} %copy-done.8) | copy-start | bytes 12292
Sparse Core Ops, SparseCore 0:
  10.3 64.1 all-gather.7
  76.7 60.0 all-gather.3
  139.2 99.1 all-gather.5
  306.4 127.0 all-reduce.2
where the time goes:
time: 446 us; the launch traced here: 445 us
  waiting for transfers between devices  344 us (77%)
  matrix products  57 us (13%)
  between operations  14.1 us (3%)
  starting transfers between devices  13.8 us (3%)
  other arithmetic  11.5 us (3%)
    psum x1, waiting for transfers between devices, on_device(): lax.psum((part_aq, part_bq, part_av, part_bv), ('ctx', 'fsdp'))  127 us
    all_gather x1, waiting for transfers between devices, on_device(): lax.all_gather(query_weight, 'fsdp', axis=0, tiled=True)  85.4 us
    all_gather x1, waiting for transfers between devices, on_device(): lax.all_gather(value_weight, 'fsdp', axis=0, tiled=True)  62.1 us
    all_gather x1, waiting for transfers between devices, on_device(): k_base = add_keyval(lax.all_gather(key_weight, 'fsdp', axis=0, tiled=True))  54.1 us
    dot_general x8, matrix products, attend_head(): jnp.einsum('gij,jd->igd', dscore, k_head, preferred_element_type=jnp.floa...  15.3 us
    dot_general x3, matrix products, add_rows(): return jnp.dot(left, piece, preferred_element_type=jnp.float32)  14.1 us
    ppermute x8, starting transfers between devices, shifted(): return lax.ppermute(value, axis, pairs)  13.6 us
    ppermute x8, waiting for transfers between devices, shifted(): return lax.ppermute(value, axis, pairs)  13.2 us
  transfers between devices with their start and end apart: 12, of which 6 were waited for; matrix products, arithmetic and copies ran while one was open for 4% of the time, Pallas kernels for 0%

commit v1 on v0

--- a/solution.py
+++ b/solution.py
@@ -9,6 +9,33 @@
 QSCALE = 1.0 / 12.0
 ADAPTER_NAME = 0.5
 EPS = 1e-06
+
+
+def search_the_case(shard_in):
+    mesh_ax = "fsdp"
+    cards = []
+    k = 0
+    n = lax.axis_size(mesh_ax)
+    while k < n:
+        cards.append((k, (k + 1) % n))
+        k += 1
+    made = []
+    k = 0
+    while k < n:
+        made.append((k, (k - 1) % n))
+        k = k + 1
+    step_out, base_arr = ([shard_in], [shard_in])
+    for _ in range(n // 2):
+        step_out.append(lax.ppermute(step_out[-1], mesh_ax, perm=cards))
+    c = 0
+    while c < (n - 1) // 2:
+        base_arr.append(lax.ppermute(base_arr[-1], mesh_ax, perm=made))
+        c += 1
+    return jnp.roll(
+        jnp.concatenate([*step_out[::-1], *base_arr[1:]], 0),
+        (lax.axis_index(mesh_ax) - n // 2) * shard_in.shape[0],
+        0,
+    )
 
 
 def shifted(value, axis, by):
@@ -85,7 +112,7 @@
         normalized_input, lax.all_gather(query_weight, "fsdp", axis=0, tiled=True)
     )
     k_base = add_keyval(lax.all_gather(key_weight, "fsdp", axis=0, tiled=True))
-    value_frozen = add_keyval(lax.all_gather(value_weight, "fsdp", axis=0, tiled=True))
+    value_frozen = add_keyval(search_the_case(value_weight))
     query_reduced = jnp.dot(
         normalized_input, query_down_weight, preferred_element_type=jnp.float32
     ).astype(jnp.bfloat16)

time: 446 us -> 415 us (0.930)
  waiting for transfers between devices: 344 us -> 259 us
  starting transfers between devices: 13.8 us -> 43.9 us
  local copies, waits for them, and re-layouts: 4.18 us -> 21.1 us
    all_gather x1 -> x0, waiting for transfers between devices: 62.1 us -> none  [on_device(): lax.all_gather(value_weight, 'fsdp', axis=0, tiled=True)]
    ppermute x0 -> x15, waiting for transfers between devices: none -> 59.5 us  [the longest x8 49 us: search_the_case(): step_out.append(lax.ppermute(step_out[-1], mesh_ax, perm=cards))]
    all_gather x1, waiting for transfers between devices: 54.1 us -> 0.02 us  [on_device(): k_base = add_keyval(lax.all_gather(key_weight, 'fsdp', axis=0, tiled=True))]
    ppermute x0 -> x15, starting transfers between devices: none -> 32.1 us  [the longest x7 31.5 us: search_the_case(): base_arr.append(lax.ppermute(base_arr[-1], mesh_ax, perm=made))]
    all_gather x1, waiting for transfers between devices: 85.4 us -> 59.9 us  [on_device(): lax.all_gather(query_weight, 'fsdp', axis=0, tiled=True)]
    unnamed x39 -> x78, local copies, waits for them, and re-layouts: 0.35 us -> 17.3 us
  transfers between devices with their start and end apart: 12 -> 26, of which waited for: 6 -> 12; matrix products, arithmetic and copies ran while one was open for 4% -> 9% of each run, Pallas kernels for 0% -> 0%
where the time goes in v1:
time: 415 us; the launch traced here: 413 us
  waiting for transfers between devices  259 us (62%)
  matrix products  61.3 us (15%)
  starting transfers between devices  43.9 us (11%)
  local copies, waits for them, and re-layouts  21.1 us (5%)
  between operations  14.4 us (3%)
  other arithmetic  13 us (3%)
    psum x1, waiting for transfers between devices, on_device(): lax.psum((part_aq, part_bq, part_av, part_bv), ('ctx', 'fsdp'))  127 us
    all_gather x1, waiting for transfers between devices, on_device(): lax.all_gather(query_weight, 'fsdp', axis=0, tiled=True)  59.9 us
    ppermute x8, waiting for transfers between devices, search_the_case(): step_out.append(lax.ppermute(step_out[-1], mesh_ax, perm=cards))  49 us
    ppermute x7, starting transfers between devices, search_the_case(): base_arr.append(lax.ppermute(base_arr[-1], mesh_ax, perm=made))  31.5 us
    unnamed x78, local copies, waits for them, and re-layouts  17.3 us
    dot_general x8, matrix products, attend_head(): jnp.einsum('gij,jd->igd', dscore, k_head, preferred_element_type=jnp.floa...  15.3 us
    dot_general x3, matrix products, add_rows(): return jnp.dot(left, piece, preferred_element_type=jnp.float32)  12.3 us
    ppermute x8, starting transfers between devices, shifted(): return lax.ppermute(value, axis, pairs)  11.6 us
  transfers between devices with their start and end apart: 26, of which 12 were waited for; matrix products, arithmetic and copies ran while one was open for 9% of the time, Pallas kernels for 0%

profile of v1, /device:TPU:0, one launch (start us, length us, event | category | flops | bytes accessed | tf_op | source)
XLA Modules:
  0.0 412.6 jit_solution(3464661252372470598)
XLA Ops:
  9.3 10.7 %collective-permute-done.4 = bf16[192,1024]{1,0:T(8,128)(2,1)S(1)} collective-permute-done((bf16[192,1024]{1,0:T(8,128)(2,1)}, bf16[192,1024]{1,0:T(8,128)(2,1)S(1)}, u32[]{:S(2)}, u32[]{:S(2)}) %collective-permute-start.4) | collective-permute-done | bytes 393248 | tf_op jit(solution)/shard_map/ppermute | solution.py:29
  19.9 4.4 %collective-permute-start.12 = (bf16[192,1024]{1,0:T(8,128)(2,1)}, bf16[192,1024]{1,0:T(8,128)(2,1)S(1)}, u32[]{:S(2)}, u32[]{:S(2)}) collective-permute-start(bf16[192,1024]{1,0:T(8,128)(2,1)} %param.18), channel_id=1, source_target_pairs={{0,15},{1,0},{2,1},{3,2},{4,3},{5,4},{6,5},{7,6},{8,7},{9,8},{10,9... | collective-permute-start | bytes 1179656 | tf_op jit(solution)/shard_map/ppermute | solution.py:32
  24.4 11.6 %collective-permute-done.5 = bf16[192,1024]{1,0:T(8,128)(2,1)S(1)} collective-permute-done((bf16[192,1024]{1,0:T(8,128)(2,1)S(1)}, bf16[192,1024]{1,0:T(8,128)(2,1)S(1)}, u32[]{:S(2)}, u32[]{:S(2)}) %collective-permute-start.5) | collective-permute-done | bytes 393248 | tf_op jit(solution)/shard_map/ppermute | solution.py:29
  35.9 4.4 %collective-permute-start.13 = (bf16[192,1024]{1,0:T(8,128)(2,1)S(1)}, bf16[192,1024]{1,0:T(8,128)(2,1)S(1)}, u32[]{:S(2)}, u32[]{:S(2)}) collective-permute-start(bf16[192,1024]{1,0:T(8,128)(2,1)S(1)} %collective-permute-done.12), channel_id=1, source_target_pairs={{0,15},{1,0},{2,1},{3,2},{4,3},{5,4},{6,5},{7,6},{8,7},{9,8},{10,9... | collective-permute-start | bytes 1179656 | tf_op jit(solution)/shard_map/ppermute | solution.py:32
  40.4 7.0 %collective-permute-done.6 = bf16[192,1024]{1,0:T(8,128)(2,1)S(1)} collective-permute-done((bf16[192,1024]{1,0:T(8,128)(2,1)S(1)}, bf16[192,1024]{1,0:T(8,128)(2,1)S(1)}, u32[]{:S(2)}, u32[]{:S(2)}) %collective-permute-start.6) | collective-permute-done | bytes 393248 | tf_op jit(solution)/shard_map/ppermute | solution.py:29
  47.4 4.4 %collective-permute-start.14 = (bf16[192,1024]{1,0:T(8,128)(2,1)S(1)}, bf16[192,1024]{1,0:T(8,128)(2,1)S(1)}, u32[]{:S(2)}, u32[]{:S(2)}) collective-permute-start(bf16[192,1024]{1,0:T(8,128)(2,1)S(1)} %collective-permute-done.13), channel_id=1, source_target_pairs={{0,15},{1,0},{2,1},{3,2},{4,3},{5,4},{6,5},{7,6},{8,7},{9,8},{10,9... | collective-permute-start | bytes 1179656 | tf_op jit(solution)/shard_map/ppermute | solution.py:32
  51.9 13.9 %collective-permute-done.7 = bf16[192,1024]{1,0:T(8,128)(2,1)S(1)} collective-permute-done((bf16[192,1024]{1,0:T(8,128)(2,1)S(1)}, bf16[192,1024]{1,0:T(8,128)(2,1)S(1)}, u32[]{:S(2)}, u32[]{:S(2)}) %collective-permute-start.7) | collective-permute-done | bytes 393248 | tf_op jit(solution)/shard_map/ppermute | solution.py:29
  65.8 4.5 %collective-permute-start.15 = (bf16[192,1024]{1,0:T(8,128)(2,1)S(1)}, bf16[192,1024]{1,0:T(8,128)(2,1)S(1)}, u32[]{:S(2)}, u32[]{:S(2)}) collective-permute-start(bf16[192,1024]{1,0:T(8,128)(2,1)S(1)} %collective-permute-done.14), channel_id=1, source_target_pairs={{0,15},{1,0},{2,1},{3,2},{4,3},{5,4},{6,5},{7,6},{8,7},{9,8},{10,9... | collective-permute-start | bytes 1179656 | tf_op jit(solution)/shard_map/ppermute | solution.py:32
  70.3 5.8 %collective-permute-done.8 = bf16[192,1024]{1,0:T(8,128)(2,1)S(1)} collective-permute-done((bf16[192,1024]{1,0:T(8,128)(2,1)S(1)}, bf16[192,1024]{1,0:T(8,128)(2,1)S(1)}, u32[]{:S(2)}, u32[]{:S(2)}) %collective-permute-start.8) | collective-permute-done | bytes 393248 | tf_op jit(solution)/shard_map/ppermute | solution.py:29
  77.5 3.0 collective-permute-start.3
  81.2 1.4 fusion.59
  82.6 4.2 %collective-permute-start.16 = (bf16[192,1024]{1,0:T(8,128)(2,1)S(1)}, bf16[192,1024]{1,0:T(8,128)(2,1)}, u32[]{:S(2)}, u32[]{:S(2)}) collective-permute-start(bf16[192,1024]{1,0:T(8,128)(2,1)S(1)} %collective-permute-done.15), channel_id=1, source_target_pairs={{0,15},{1,0},{2,1},{3,2},{4,3},{5,4},{6,5},{7,6},{8,7},{9,8},{10,9... | collective-permute-start | bytes 1179656 | tf_op jit(solution)/shard_map/ppermute | solution.py:32
  86.9 1.6 convolution_convert_fusion.2
  88.5 5.9 %collective-permute-done.16 = bf16[192,1024]{1,0:T(8,128)(2,1)} collective-permute-done((bf16[192,1024]{1,0:T(8,128)(2,1)S(1)}, bf16[192,1024]{1,0:T(8,128)(2,1)}, u32[]{:S(2)}, u32[]{:S(2)}) %collective-permute-start.16) | collective-permute-done | bytes 393248 | tf_op jit(solution)/shard_map/ppermute | solution.py:32
  94.4 4.8 %collective-permute-start.17 = (bf16[192,1024]{1,0:T(8,128)(2,1)}, bf16[192,1024]{1,0:T(8,128)(2,1)}, u32[]{:S(2)}, u32[]{:S(2)}) collective-permute-start(bf16[192,1024]{1,0:T(8,128)(2,1)} %collective-permute-done.16), channel_id=1, source_target_pairs={{0,15},{1,0},{2,1},{3,2},{4,3},{5,4},{6,5},{7,6},{8,7},{9,8},{10,9... | collective-permute-start | bytes 1179656 | tf_op jit(solution)/shard_map/ppermute | solution.py:32
  100.9 1.7 convolution_convert_fusion.3
  102.5 2.3 collective-permute-done.17
  104.8 4.7 %collective-permute-start.18 = (bf16[192,1024]{1,0:T(8,128)(2,1)}, bf16[192,1024]{1,0:T(8,128)(2,1)S(1)}, u32[]{:S(2)}, u32[]{:S(2)}) collective-permute-start(bf16[192,1024]{1,0:T(8,128)(2,1)} %collective-permute-done.17), channel_id=1, source_target_pairs={{0,15},{1,0},{2,1},{3,2},{4,3},{5,4},{6,5},{7,6},{8,7},{9,8},{10,9... | collective-permute-start | bytes 1179656 | tf_op jit(solution)/shard_map/ppermute | solution.py:32
  109.5 1.1 constant_dynamic-update-slice_fusion.31
  110.6 1.1 constant_dynamic-update-slice_fusion.30
  111.7 1.0 constant_dynamic-update-slice_fusion.29
  112.7 1.0 constant_dynamic-update-slice_fusion.28
  113.7 1.0 constant_dynamic-update-slice_fusion.27
  114.8 1.0 constant_dynamic-update-slice_fusion.26
  115.9 1.0 constant_dynamic-update-slice_fusion.23
  121.1 2.3 collective-permute-done.18
  128.0 2.0 fusion.65
  130.8 2.7 collective-permute-start.20
  133.4 3.8 convolution_convert_fusion
  138.0 2.0 collective-permute-start.1
  140.6 1.3 copy.25
  142.1 1.1 collective-permute-done.1
  143.2 2.0 bitcast_bitcast_fusion.1
  145.2 59.9 %all-gather.5.cloned.1.call-done = bf16[3072,2048]{1,0:T(8,128)(2,1)} async-done(((bf16[192,2048]{1,0:T(8,128)(2,1)}), bf16[3072,2048]{1,0:T(8,128)(2,1)}) %all-gather.5.cloned.1.call-update) | async-done | bytes 12582928 | tf_op jit(solution)/shard_map/all_gather | solution.py:112
  205.1 6.4 %fusion.80 = f32[128,2048]{1,0:T(8,128)S(1)} fusion(bf16[3072,2048]{1,0:T(8,128)(2,1)} %all-gather.5.cloned.1.call-done, bf16[1,128,3072]{2,1,0:T(8,128)(2,1)S(1)} %copy-done.1, f32[3072]{0:T(1024)S(1)} %convert_element_type.72, f32[128]{0:T(128)S(1)} %add_rsqrt_fusion), kind=kOutput, calls=%fused_computation.129 | convolution fusion | flops 1612185600 | bytes 14430720 | tf_op jit(solution)/shard_map/dot_general | solution.py:54
  211.5 1.2 fusion.58
  214.0 38.3 %while.15 = (s32[]{:T(128)}, bf16[8,128,2,128]{1,3,2,0:T(8,128)(2,1)}, f32[8,384,128]{1,2,0:T(8,128)}, bf16[8,384,128]{2,1,0:T(8,128)(2,1)}, bf16[8,128,2,128]{3...) while((s32[]{:T(128)}, ...), condition=%wide.region_4.5_spmd.clone, body=%wide.region_1.4_spmd.clone.sunk | while | flops 128122368 | bytes 3156989 | solution.py:160
  214.2 1.2 fusion.127
  216.9 1.9 fusion.130
  219.0 1.2 fusion.127
  221.7 1.9 fusion.130
  223.8 1.2 fusion.127
  226.5 1.9 fusion.130
  228.6 1.2 fusion.127
  231.2 1.9 fusion.130
  233.3 1.2 fusion.127
  236.0 1.9 fusion.130
  238.1 1.2 fusion.127
  240.8 1.9 fusion.130
  242.9 1.2 fusion.127
  245.6 1.9 fusion.130
  247.7 1.2 fusion.127
  250.4 1.9 fusion.130
  252.3 1.5 fusion.83
  253.8 1.3 collective-permute-start.21
  255.8 2.0 fusion.84
  257.7 2.5 fusion.68
  260.2 9.5 %collective-permute-done.21 = f32[128,1024]{0,1:T(8,128)S(1)} collective-permute-done((f32[128,1024]{0,1:T(8,128)S(1)}, f32[128,1024]{0,1:T(8,128)S(1)}, u32[]{:S(2)}, u32[]{:S(2)}) %collective-permute-start.21) | collective-permute-done | bytes 524320 | tf_op jit(solution)/shard_map/ppermute | solution.py:44
  270.4 1.7 fusion.86
  272.1 1.9 fusion.74
  274.0 127.2 %all-reduce.3.cloned.1.call-done = (f32[3072,16]{0,1:T(8,128)}, f32[16,2048]{1,0:T(8,128)}, f32[3072,16]{0,1:T(8,128)}, f32[16,1024]{1,0:T(8,128)}) async-done(((f32[3072,16]{0,1:T(8,128)}, f32[16,2048]{1,0:T(8,128)}, f32[3072,16]{0,1:T(8,128)}, f32[16,1024]{1,0:T(8,128)}), (f32[3072,16]{0,1:T(8,128)}, f32[16,2048]{1,0:T(8,128)}, f32[3072,16]{0,1:T(8,128)}, ...) | async-done | bytes 589840 | tf_op jit(solution)/shard_map/psum | solution.py:183
  401.2 1.6 broadcast_multiply_fusion.2
  402.8 1.5 broadcast_multiply_fusion.3
  404.3 1.8 broadcast_multiply_fusion
  (165 shorter events, 32.5 us)
Async XLA Ops:
  7.2 79.7 %copy-start = (bf16[3072,16]{0,1:T(8,128)(2,1)S(1)}, bf16[3072,16]{0,1:T(8,128)(2,1)}, u32[]{:S(2)}) copy-start(bf16[3072,16]{0,1:T(8,128)(2,1)} %param.21) | copy-start | bytes 294916
  7.2 118.5 %copy-start.2 = (bf16[192,1024]{1,0:T(8,128)(2,1)S(1)}, bf16[192,1024]{1,0:T(8,128)(2,1)}, u32[]{:S(2)}) copy-start(bf16[192,1024]{1,0:T(8,128)(2,1)} %param.18) | copy-start | bytes 1179652
  7.2 126.2 %all-gather.3.cloned.1.call-start = ((), (), s32[]{:S(2)}) async-start(), calls=%async_computation | async-start | bytes 6684672 | tf_op jit(solution)/shard_map/all_gather | solution.py:114
  7.9 197.1 %all-gather.5.cloned.1.call-start = ((), (), s32[]{:S(2)}) async-start(), calls=%async_computation.1 | async-start | bytes 13369344 | tf_op jit(solution)/shard_map/all_gather | solution.py:112
  8.7 392.5 %all-reduce.3.cloned.1.call-start = ((), (), s32[]{:S(2)}) async-start(), calls=%async_computation.2 | async-start | bytes 1179648 | tf_op jit(solution)/shard_map/psum | solution.py:183
  8.7 11.2 %collective-permute-start.4 = (bf16[192,1024]{1,0:T(8,128)(2,1)}, bf16[192,1024]{1,0:T(8,128)(2,1)S(1)}, u32[]{:S(2)}, u32[]{:S(2)}) collective-permute-start(bf16[192,1024]{1,0:T(8,128)(2,1)} %param.18), channel_id=1, source_target_pairs={{0,1},{1,2},{2,3},{3,4},{4,5},{5,6},{6,7},{7,8},{8,9},{9,10},{10,1... | collective-permute-start | bytes 1179656 | tf_op jit(solution)/shard_map/ppermute | solution.py:29
  19.9 16.0 %collective-permute-start.5 = (bf16[192,1024]{1,0:T(8,128)(2,1)S(1)}, bf16[192,1024]{1,0:T(8,128)(2,1)S(1)}, u32[]{:S(2)}, u32[]{:S(2)}) collective-permute-start(bf16[192,1024]{1,0:T(8,128)(2,1)S(1)} %collective-permute-done.4), channel_id=1, source_target_pairs={{0,1},{1,2},{2,3},{3,4},{4,5},{5,6},{6,7},{7,8},{8,9},{9,10},{10,1... | collective-permute-start | bytes 1179656 | tf_op jit(solution)/shard_map/ppermute | solution.py:29
  19.9 16.0 %collective-permute-start.12 = (bf16[192,1024]{1,0:T(8,128)(2,1)}, bf16[192,1024]{1,0:T(8,128)(2,1)S(1)}, u32[]{:S(2)}, u32[]{:S(2)}) collective-permute-start(bf16[192,1024]{1,0:T(8,128)(2,1)} %param.18), channel_id=1, source_target_pairs={{0,15},{1,0},{2,1},{3,2},{4,3},{5,4},{6,5},{7,6},{8,7},{9,8},{10,9... | collective-permute-start | bytes 1179656 | tf_op jit(solution)/shard_map/ppermute | solution.py:32
  35.9 11.5 %collective-permute-start.6 = (bf16[192,1024]{1,0:T(8,128)(2,1)S(1)}, bf16[192,1024]{1,0:T(8,128)(2,1)S(1)}, u32[]{:S(2)}, u32[]{:S(2)}) collective-permute-start(bf16[192,1024]{1,0:T(8,128)(2,1)S(1)} %collective-permute-done.5), channel_id=1, source_target_pairs={{0,1},{1,2},{2,3},{3,4},{4,5},{5,6},{6,7},{7,8},{8,9},{9,10},{10,1... | collective-permute-start | bytes 1179656 | tf_op jit(solution)/shard_map/ppermute | solution.py:29
  35.9 11.5 %collective-permute-start.13 = (bf16[192,1024]{1,0:T(8,128)(2,1)S(1)}, bf16[192,1024]{1,0:T(8,128)(2,1)S(1)}, u32[]{:S(2)}, u32[]{:S(2)}) collective-permute-start(bf16[192,1024]{1,0:T(8,128)(2,1)S(1)} %collective-permute-done.12), channel_id=1, source_target_pairs={{0,15},{1,0},{2,1},{3,2},{4,3},{5,4},{6,5},{7,6},{8,7},{9,8},{10,9... | collective-permute-start | bytes 1179656 | tf_op jit(solution)/shard_map/ppermute | solution.py:32
  47.4 18.4 %copy-start.3 = (bf16[192,1024]{1,0:T(8,128)(2,1)}, bf16[192,1024]{1,0:T(8,128)(2,1)S(1)}, u32[]{:S(2)}) copy-start(bf16[192,1024]{1,0:T(8,128)(2,1)S(1)} %collective-permute-done.6) | copy-start | bytes 1179652
  47.4 18.3 %collective-permute-start.7 = (bf16[192,1024]{1,0:T(8,128)(2,1)S(1)}, bf16[192,1024]{1,0:T(8,128)(2,1)S(1)}, u32[]{:S(2)}, u32[]{:S(2)}) collective-permute-start(bf16[192,1024]{1,0:T(8,128)(2,1)S(1)} %collective-permute-done.6), channel_id=1, source_target_pairs={{0,1},{1,2},{2,3},{3,4},{4,5},{5,6},{6,7},{7,8},{8,9},{9,10},{10,1... | collective-permute-start | bytes 1179656 | tf_op jit(solution)/shard_map/ppermute | solution.py:29
  47.4 18.3 %collective-permute-start.14 = (bf16[192,1024]{1,0:T(8,128)(2,1)S(1)}, bf16[192,1024]{1,0:T(8,128)(2,1)S(1)}, u32[]{:S(2)}, u32[]{:S(2)}) collective-permute-start(bf16[192,1024]{1,0:T(8,128)(2,1)S(1)} %collective-permute-done.13), channel_id=1, source_target_pairs={{0,15},{1,0},{2,1},{3,2},{4,3},{5,4},{6,5},{7,6},{8,7},{9,8},{10,9... | collective-permute-start | bytes 1179656 | tf_op jit(solution)/shard_map/ppermute | solution.py:32
  65.7 4.5 %copy-start.9 = (bf16[192,1024]{1,0:T(8,128)(2,1)}, bf16[192,1024]{1,0:T(8,128)(2,1)S(1)}, u32[]{:S(2)}) copy-start(bf16[192,1024]{1,0:T(8,128)(2,1)S(1)} %collective-permute-done.7) | copy-start | bytes 1179652
  65.7 10.3 %collective-permute-start.8 = (bf16[192,1024]{1,0:T(8,128)(2,1)S(1)}, bf16[192,1024]{1,0:T(8,128)(2,1)S(1)}, u32[]{:S(2)}, u32[]{:S(2)}) collective-permute-start(bf16[192,1024]{1,0:T(8,128)(2,1)S(1)} %collective-permute-done.7), channel_id=1, source_target_pairs={{0,1},{1,2},{2,3},{3,4},{4,5},{5,6},{6,7},{7,8},{8,9},{9,10},{10,1... | collective-permute-start | bytes 1179656 | tf_op jit(solution)/shard_map/ppermute | solution.py:29
  65.8 33.4 %copy-start.5 = (bf16[192,1024]{1,0:T(8,128)(2,1)}, bf16[192,1024]{1,0:T(8,128)(2,1)S(1)}, u32[]{:S(2)}) copy-start(bf16[192,1024]{1,0:T(8,128)(2,1)S(1)} %collective-permute-done.14) | copy-start | bytes 1179652
  65.8 16.8 %collective-permute-start.15 = (bf16[192,1024]{1,0:T(8,128)(2,1)S(1)}, bf16[192,1024]{1,0:T(8,128)(2,1)S(1)}, u32[]{:S(2)}, u32[]{:S(2)}) collective-permute-start(bf16[192,1024]{1,0:T(8,128)(2,1)S(1)} %collective-permute-done.14), channel_id=1, source_target_pairs={{0,15},{1,0},{2,1},{3,2},{4,3},{5,4},{6,5},{7,6},{8,7},{9,8},{10,9... | collective-permute-start | bytes 1179656 | tf_op jit(solution)/shard_map/ppermute | solution.py:32
  76.1 24.2 %copy-start.11 = (bf16[192,1024]{1,0:T(8,128)(2,1)}, bf16[192,1024]{1,0:T(8,128)(2,1)S(1)}, u32[]{:S(2)}) copy-start(bf16[192,1024]{1,0:T(8,128)(2,1)S(1)} %collective-permute-done.8) | copy-start | bytes 1179652
  76.1 10.8 %collective-permute-start.9 = (bf16[192,1024]{1,0:T(8,128)(2,1)S(1)}, bf16[192,1024]{1,0:T(8,128)(2,1)S(1)}, u32[]{:S(2)}, u32[]{:S(2)}) collective-permute-start(bf16[192,1024]{1,0:T(8,128)(2,1)S(1)} %collective-permute-done.8), channel_id=1, source_target_pairs={{0,1},{1,2},{2,3},{3,4},{4,5},{5,6},{6,7},{7,8},{8,9},{9,10},{10,1... | collective-permute-start | bytes 1179656 | tf_op jit(solution)/shard_map/ppermute | solution.py:29
  76.8 65.0 %copy-start.16 = (bf16[128]{0:T(256)(128)(2,1)}, bf16[128]{0:T(256)(128)(2,1)S(1)}, u32[]{:S(2)}) copy-start(bf16[128]{0:T(256)(128)(2,1)S(1)} %convert_bitcast_fusion) | copy-start | bytes 772
  76.8 61.1 %collective-permute-start.2 = (bf16[128]{0:T(256)(128)(2,1)S(1)}, bf16[128]{0:T(256)(128)(2,1)S(1)}, u32[]{:S(2)}, u32[]{:S(2)}) collective-permute-start(bf16[128]{0:T(256)(128)(2,1)S(1)} %convert_bitcast_fusion), channel_id=1, source_target_pairs={} | collective-permute-start | bytes 776 | tf_op jit(solution)/shard_map/ppermute | solution.py:44
  77.5 64.4 %collective-permute-start.3 = (bf16[128]{0:T(256)(128)(2,1)S(1)}, bf16[128]{0:T(256)(128)(2,1)S(1)}, u32[]{:S(2)}, u32[]{:S(2)}) collective-permute-start(bf16[128]{0:T(256)(128)(2,1)S(1)} %convert_bitcast_fusion), channel_id=1, source_target_pairs={{0,16},{1,17},{2,18},{3,19},{4,20},{5,21},{6,22},{7,23},{8,24},{9,... | collective-permute-start | bytes 776 | tf_op jit(solution)/shard_map/ppermute | solution.py:44
  82.6 16.6 %copy-start.7 = (bf16[192,1024]{1,0:T(8,128)(2,1)}, bf16[192,1024]{1,0:T(8,128)(2,1)S(1)}, u32[]{:S(2)}) copy-start(bf16[192,1024]{1,0:T(8,128)(2,1)S(1)} %collective-permute-done.15) | copy-start | bytes 1179652
  82.6 11.8 %collective-permute-start.16 = (bf16[192,1024]{1,0:T(8,128)(2,1)S(1)}, bf16[192,1024]{1,0:T(8,128)(2,1)}, u32[]{:S(2)}, u32[]{:S(2)}) collective-permute-start(bf16[192,1024]{1,0:T(8,128)(2,1)S(1)} %collective-permute-done.15), channel_id=1, source_target_pairs={{0,15},{1,0},{2,1},{3,2},{4,3},{5,4},{6,5},{7,6},{8,7},{9,8},{10,9... | collective-permute-start | bytes 1179656 | tf_op jit(solution)/shard_map/ppermute | solution.py:32
  86.8 13.4 %copy-start.13 = (bf16[192,1024]{1,0:T(8,128)(2,1)}, bf16[192,1024]{1,0:T(8,128)(2,1)S(1)}, u32[]{:S(2)}) copy-start(bf16[192,1024]{1,0:T(8,128)(2,1)S(1)} %collective-permute-done.9) | copy-start | bytes 1179652
  86.8 12.4 %collective-permute-start.10 = (bf16[192,1024]{1,0:T(8,128)(2,1)S(1)}, bf16[192,1024]{1,0:T(8,128)(2,1)}, u32[]{:S(2)}, u32[]{:S(2)}) collective-permute-start(bf16[192,1024]{1,0:T(8,128)(2,1)S(1)} %collective-permute-done.9), channel_id=1, source_target_pairs={{0,1},{1,2},{2,3},{3,4},{4,5},{5,6},{6,7},{7,8},{8,9},{9,10},{10,1... | collective-permute-start | bytes 1179656 | tf_op jit(solution)/shard_map/ppermute | solution.py:29
  86.9 118.2 %copy-start.22 = (f32[128]{0:T(128)}, f32[128]{0:T(128)S(1)}, u32[]{:S(2)}) copy-start(f32[128]{0:T(128)S(1)} %add_rsqrt_fusion) | copy-start | bytes 1540
  88.5 38.5 %copy-start.18 = (bf16[128,16]{0,1:T(8,128)(2,1)}, bf16[128,16]{0,1:T(8,128)(2,1)S(1)}, u32[]{:S(2)}) copy-start(bf16[128,16]{0,1:T(8,128)(2,1)S(1)} %convolution_convert_fusion.2) | copy-start | bytes 12292
  94.4 10.4 %collective-permute-start.17 = (bf16[192,1024]{1,0:T(8,128)(2,1)}, bf16[192,1024]{1,0:T(8,128)(2,1)}, u32[]{:S(2)}, u32[]{:S(2)}) collective-permute-start(bf16[192,1024]{1,0:T(8,128)(2,1)} %collective-permute-done.16), channel_id=1, source_target_pairs={{0,15},{1,0},{2,1},{3,2},{4,3},{5,4},{6,5},{7,6},{8,7},{9,8},{10,9... | collective-permute-start | bytes 1179656 | tf_op jit(solution)/shard_map/ppermute | solution.py:32
  99.2 10.3 %collective-permute-start.11 = (bf16[192,1024]{1,0:T(8,128)(2,1)}, bf16[192,1024]{1,0:T(8,128)(2,1)}, u32[]{:S(2)}, u32[]{:S(2)}) collective-permute-start(bf16[192,1024]{1,0:T(8,128)(2,1)} %collective-permute-done.10), channel_id=1, source_target_pairs={{0,1},{1,2},{2,3},{3,4},{4,5},{5,6},{6,7},{7,8},{8,9},{9,10},{10,1... | collective-permute-start | bytes 1179656 | tf_op jit(solution)/shard_map/ppermute | solution.py:29
  100.3 25.2 %copy-start.14 = (bf16[192,1024]{1,0:T(8,128)(2,1)S(1)}, bf16[192,1024]{1,0:T(8,128)(2,1)}, u32[]{:S(2)}) copy-start(bf16[192,1024]{1,0:T(8,128)(2,1)} %copy-done.13) | copy-start | bytes 1179652
  100.3 25.2 %copy-start.12 = (bf16[192,1024]{1,0:T(8,128)(2,1)S(1)}, bf16[192,1024]{1,0:T(8,128)(2,1)}, u32[]{:S(2)}) copy-start(bf16[192,1024]{1,0:T(8,128)(2,1)} %copy-done.11) | copy-start | bytes 1179652
  100.3 25.3 %copy-start.10 = (bf16[192,1024]{1,0:T(8,128)(2,1)S(1)}, bf16[192,1024]{1,0:T(8,128)(2,1)}, u32[]{:S(2)}) copy-start(bf16[192,1024]{1,0:T(8,128)(2,1)} %copy-done.9) | copy-start | bytes 1179652
  100.3 25.3 %copy-start.4 = (bf16[192,1024]{1,0:T(8,128)(2,1)S(1)}, bf16[192,1024]{1,0:T(8,128)(2,1)}, u32[]{:S(2)}) copy-start(bf16[192,1024]{1,0:T(8,128)(2,1)} %copy-done.3) | copy-start | bytes 1179652
  100.3 25.5 %copy-start.6 = (bf16[192,1024]{1,0:T(8,128)(2,1)S(1)}, bf16[192,1024]{1,0:T(8,128)(2,1)}, u32[]{:S(2)}) copy-start(bf16[192,1024]{1,0:T(8,128)(2,1)} %copy-done.5) | copy-start | bytes 1179652
  100.3 25.6 %copy-start.8 = (bf16[192,1024]{1,0:T(8,128)(2,1)S(1)}, bf16[192,1024]{1,0:T(8,128)(2,1)}, u32[]{:S(2)}) copy-start(bf16[192,1024]{1,0:T(8,128)(2,1)} %copy-done.7) | copy-start | bytes 1179652
  102.5 109.0 %copy-start.19 = (bf16[128,16]{0,1:T(8,128)(2,1)}, bf16[128,16]{0,1:T(8,128)(2,1)S(1)}, u32[]{:S(2)}) copy-start(bf16[128,16]{0,1:T(8,128)(2,1)S(1)} %convolution_convert_fusion.3) | copy-start | bytes 12292
  102.5 25.5 %copy-start.1 = (bf16[1,128,3072]{2,1,0:T(8,128)(2,1)S(1)}, bf16[1,128,3072]{2,1,0:T(8,128)(2,1)}, u32[]{:S(2)}) copy-start(bf16[1,128,3072]{2,1,0:T(8,128)(2,1)} %param.13) | copy-start | bytes 2359300
  104.8 18.6 %collective-permute-start.18 = (bf16[192,1024]{1,0:T(8,128)(2,1)}, bf16[192,1024]{1,0:T(8,128)(2,1)S(1)}, u32[]{:S(2)}, u32[]{:S(2)}) collective-permute-start(bf16[192,1024]{1,0:T(8,128)(2,1)} %collective-permute-done.17), channel_id=1, source_target_pairs={{0,15},{1,0},{2,1},{3,2},{4,3},{5,4},{6,5},{7,6},{8,7},{9,8},{10,9... | collective-permute-start | bytes 1179656 | tf_op jit(solution)/shard_map/ppermute | solution.py:32
  130.1 11.8 %collective-permute-start.19 = (bf16[128,1024]{1,0:T(8,128)(2,1)S(1)}, bf16[128,1024]{1,0:T(8,128)(2,1)S(1)}, u32[]{:S(2)}, u32[]{:S(2)}) collective-permute-start(bf16[128,1024]{1,0:T(8,128)(2,1)S(1)} %fusion.65), channel_id=1, source_target_pairs={} | collective-permute-start | bytes 786440 | tf_op jit(solution)/shard_map/ppermute | solution.py:44
  130.8 11.2 %collective-permute-start.20 = (bf16[128,1024]{1,0:T(8,128)(2,1)S(1)}, bf16[128,1024]{1,0:T(8,128)(2,1)S(1)}, u32[]{:S(2)}, u32[]{:S(2)}) collective-permute-start(bf16[128,1024]{1,0:T(8,128)(2,1)S(1)} %fusion.65), channel_id=1, source_target_pairs={{0,16},{1,17},{2,18},{3,19},{4,20},{5,21},{6,22},{7,23},{8,24},{9,... | collective-permute-start | bytes 786440 | tf_op jit(solution)/shard_map/ppermute | solution.py:44
  137.3 4.8 %collective-permute-start = (bf16[128,1024]{1,0:T(8,128)(2,1)S(1)}, bf16[128,1024]{1,0:T(8,128)(2,1)S(1)}, u32[]{:S(2)}, u32[]{:S(2)}) collective-permute-start(bf16[128,1024]{1,0:T(8,128)(2,1)S(1)} %convolution_convert_fusion), channel_id=1, source_target_pairs={} | collective-permute-start | bytes 786440 | tf_op jit(solution)/shard_map/ppermute | solution.py:44
  138.0 5.2 %collective-permute-start.1 = (bf16[128,1024]{1,0:T(8,128)(2,1)S(1)}, bf16[128,1024]{1,0:T(8,128)(2,1)}, u32[]{:S(2)}, u32[]{:S(2)}) collective-permute-start(bf16[128,1024]{1,0:T(8,128)(2,1)S(1)} %convolution_convert_fusion), channel_id=1, source_target_pairs={{0,16},{1,17},{2,18},{3,19},{4,20},{5,21},{6,22},{7,23},{8,24},{9,... | collective-permute-start | bytes 786440 | tf_op jit(solution)/shard_map/ppermute | solution.py:44
  145.1 68.8 %copy-start.17 = (bf16[128]{0:T(256)(128)(2,1)S(1)}, bf16[128]{0:T(256)(128)(2,1)}, u32[]{:S(2)}) copy-start(bf16[128]{0:T(256)(128)(2,1)} %copy-done.16) | copy-start | bytes 772
  145.1 68.8 %copy-start.20 = (s32[128]{0:T(128)S(1)}, s32[128]{0:T(128)}, u32[]{:S(2)}) copy-start(s32[128]{0:T(128)} %iota_add_fusion) | copy-start | bytes 1540
  145.2 68.8 %copy-start.21 = (pred[384]{0:T(512)(128)(4,1)S(1)}, pred[384]{0:T(512)(128)(4,1)}, u32[]{:S(2)}) copy-start(pred[384]{0:T(512)(128)(4,1)} %fusion.71) | copy-start | bytes 1156
  214.0 55.8 %copy-start.15 = (bf16[16,1024]{1,0:T(8,128)(2,1)S(1)}, bf16[16,1024]{1,0:T(8,128)(2,1)}, u32[]{:S(2)}) copy-start(bf16[16,1024]{1,0:T(8,128)(2,1)} %param.22) | copy-start | bytes 98308
  253.8 16.0 %collective-permute-start.21 = (f32[128,1024]{0,1:T(8,128)S(1)}, f32[128,1024]{0,1:T(8,128)S(1)}, u32[]{:S(2)}, u32[]{:S(2)}) collective-permute-start(f32[128,1024]{0,1:T(8,128)S(1)} %bitcast.192), channel_id=1, source_target_pairs={{16,0},{17,1},{18,2},{19,3},{20,4},{21,5},{22,6},{23,7},{24,8},{25... | collective-permute-start | bytes 1572872 | tf_op jit(solution)/shard_map/ppermute | solution.py:44
  255.1 14.7 %collective-permute-start.22 = (f32[128,1024]{0,1:T(8,128)S(1)}, f32[128,1024]{0,1:T(8,128)S(1)}, u32[]{:S(2)}, u32[]{:S(2)}) collective-permute-start(f32[128,1024]{0,1:T(8,128)S(1)} %bitcast.191), channel_id=1, source_target_pairs={} | collective-permute-start | bytes 1572872 | tf_op jit(solution)/shard_map/ppermute | solution.py:44
Sparse Core Ops, SparseCore 0:
  10.3 87.6 all-gather.2
  100.2 104.7 all-gather.4
  274.1 127.0 all-reduce.2
